TPU v7x, 32 devices: a whole 2x2x4 slice. The times are simulated.
32 devices in a mesh: dev: 32 (over z, y, x, core).
Axes of the slice: x: 2, y: 2, z: 4, core: 2. Of those that a mesh axis runs over, the one named last changes fastest.
Arguments:
- density_rows: bfloat16 [24576, 3840], P('dev')
- center_x: float32 [24576], replicated, may hold values from -0.25 to 1.25
- center_y: float32 [24576], replicated, may hold values from 0 to 1
- center_z: float32 [24576], replicated, may hold values from 0 to 1
- exponent: float32 [24576], replicated, may hold values from 0.5 to 150
- brick_blocks: int32 [32, 8], replicated, may hold values from 0 to 191, as said below
Outputs:
- potential: float32 [32, 4096], P('dev')
- ham_rows: float32 [24576, 3840], P('dev')
Inputs may be any that keep to these rules, and one draw needn't show every extreme that they name: `brick_blocks`: brick b belongs to device d = b. Its 8 entries are distinct blocks; 4 of them are owned by one of the devices d - 1, d, d + 1 (cyclically) and 2 by each of the other two, where block I is owned by device I // 6. Which of the three owns 4 changes from brick to brick. Blocks 0 and 191 touch brick 0.
All inputs are finite; a program needn't handle non-finite values.
Results may differ from a plain program's by a relative error of at most 0.00041.
Values may be sent and summed in bfloat16 or wider, within the bound.
A program may use at most 128 MiB of HBM per device.

v0:
```python
import math

import jax
import jax.numpy as jnp
from jax import lax
from jax.sharding import PartitionSpec as P

FB = 128
KB = 8
CAP = 4
BLK_DEV = 6
SIDE = 16
BR_DEV = 1


omega = 2.0 / 3.0
four_pi = 4.0 * math.pi
slater = (3.0 / math.pi) ** (1.0 / 3.0)


def extended(cells, sides, width):
    for axis, dim in sides:
        count = lax.axis_size(axis)
        head = lax.slice_in_dim(cells, 0, width, axis=dim)
        tail = lax.slice_in_dim(cells, cells.shape[dim] - width, cells.shape[dim], axis=dim)
        cells = jnp.concatenate(
            [
                lax.ppermute(tail, axis, [(i, (i + 1) % count) for i in range(count)]),
                cells,
                lax.ppermute(head, axis, [((i + 1) % count, i) for i in range(count)]),
            ],
            axis=dim,
        )
    return cells


def from_behind(value, axis, steps):
    count = lax.axis_size(axis)
    pairs = [(source, (source + steps) % count) for source in range(count)]
    return lax.ppermute(value, axis, pairs)


def periodic(distance, period):
    return jnp.mod(distance + 0.5 * period, period) - 0.5 * period


def basis_values(device, z_slot, blocks, center_x, center_y, center_z, exponent, devices):
    functions = (blocks[:, None] * FB + jnp.arange(FB, dtype=jnp.int32)[None, :]).reshape(-1)
    owner_dev = functions // (BLK_DEV * FB)
    offset = (jnp.mod(device - owner_dev + 1, devices) - 1).astype(jnp.float32)
    grid_points = (jnp.arange(SIDE, dtype=jnp.float32) + 0.5) / SIDE
    decay_rate = exponent[functions][:, None]
    along_x = offset[:, None] + grid_points[None, :] - center_x[functions][:, None]
    along_y = periodic(grid_points[None, :] - center_y[functions][:, None], 1.0)
    along_z = periodic(z_slot + grid_points[None, :] - center_z[functions][:, None], 1.0 * BR_DEV)
    factor_x = jnp.exp(-decay_rate * along_x * along_x)
    factor_y = jnp.exp(-decay_rate * along_y * along_y)
    factor_z = jnp.exp(-decay_rate * along_z * along_z)
    values = factor_x[:, :, None, None] * factor_y[:, None, :, None] * factor_z[:, None, None, :]
    return values.reshape(functions.shape[0], SIDE * SIDE * SIDE).astype(jnp.bfloat16)


def brick_basis(device, blocks, center_x, center_y, center_z, exponent, devices):
    z_slots = jnp.arange(blocks.shape[0], dtype=jnp.float32)
    return jax.vmap(
        lambda z_slot, brick_row: basis_values(
            device, z_slot, brick_row, center_x, center_y, center_z, exponent, devices
        )
    )(z_slots, blocks)


def owned_slots(blocks, holder, devices):
    owner_dev = blocks // BLK_DEV
    held_here = (owner_dev == holder).astype(jnp.int32)
    slot_rank = jnp.cumsum(held_here, axis=1) - 1
    selected = (held_here[:, None, :] == 1) & (
        slot_rank[:, None, :] == jnp.arange(CAP, dtype=jnp.int32)[None, :, None]
    )
    is_valid = jnp.any(selected, axis=2)
    slot_pick = jnp.sum(
        selected.astype(jnp.int32) * jnp.arange(KB, dtype=jnp.int32)[None, None, :], axis=2
    )
    row_blocks = jnp.take_along_axis(blocks, slot_pick, axis=1) % BLK_DEV
    col_blocks = jnp.mod(owner_dev - holder + 2, devices) * BLK_DEV + blocks % BLK_DEV
    return (slot_pick, row_blocks, col_blocks, is_valid)


def pack_rows(density_tiles, row_blocks, col_blocks, is_valid):
    full_rows = jnp.take(density_tiles, row_blocks, axis=0)
    pieces = jax.vmap(lambda rows_one, cols_one: jnp.take(rows_one, cols_one, axis=2))(
        full_rows, col_blocks
    )
    pieces = jnp.where(is_valid[:, :, None, None, None], pieces, jnp.zeros_like(pieces))
    return pieces.reshape(row_blocks.shape[0], CAP, FB, KB * FB)


def scatter_rows(ham_tiles, received, row_blocks, col_blocks):
    bricks = received.shape[0]
    pieces = received.reshape(bricks, CAP, FB, KB, FB)

    def spread(piece, cols_one):
        return jnp.zeros((FB, 5 * BLK_DEV, FB), jnp.float32).at[:, cols_one, :].add(piece)

    widened = jax.vmap(jax.vmap(spread, (0, None)), (0, 0))(pieces, col_blocks)
    return ham_tiles.at[row_blocks].add(widened)


def hartree_exchange(density, devices):
    bricks = density.shape[0]
    charge = lax.psum(jnp.sum(density), "dev")
    average = charge / (devices * bricks * density.shape[1])
    source = density - average
    sweep_one = omega * four_pi / 6.0 * source
    brick_cells = sweep_one.reshape(bricks, SIDE, SIDE, SIDE)
    padded = extended(brick_cells, (("dev", 1),), 1)
    beside_all = padded[:, 2:] + padded[:, :-2]
    beside_all = beside_all + jnp.roll(brick_cells, 1, 2) + jnp.roll(brick_cells, -1, 2)
    z_line = brick_cells.transpose(1, 2, 0, 3).reshape(SIDE, SIDE, bricks * SIDE)
    z_sum = (
        (jnp.roll(z_line, 1, 2) + jnp.roll(z_line, -1, 2))
        .reshape(SIDE, SIDE, bricks, SIDE)
        .transpose(2, 0, 1, 3)
    )
    beside_all = (beside_all + z_sum).reshape(bricks, -1)
    sweep_two = sweep_one + omega * ((four_pi * source + beside_all) / 6.0 - sweep_one)
    return sweep_two - slater * jnp.cbrt(density)


def local(density_rows, center_x, center_y, center_z, exponent, brick_blocks):
    devices = lax.axis_size("dev")
    own_index = lax.axis_index("dev")
    left_index = jnp.mod(own_index - 1, devices)
    right_index = jnp.mod(own_index + 1, devices)
    bricks = BR_DEV
    cells = SIDE * SIDE * SIDE
    scale = 64.0 / cells
    density_tiles = density_rows.reshape(BLK_DEV, FB, 5 * BLK_DEV, FB)

    def bricks_of(device):
        return lax.dynamic_slice_in_dim(brick_blocks, device * bricks, bricks, 0)

    neighbours = (left_index, own_index, right_index)
    slots_at = [owned_slots(bricks_of(device), own_index, devices) for device in neighbours]
    ham_tiles = jnp.zeros((BLK_DEV, FB, 5 * BLK_DEV, FB), jnp.float32)
    own_blocks = bricks_of(own_index)
    orbitals = brick_basis(own_index, own_blocks, center_x, center_y, center_z, exponent, devices)
    packed = [pack_rows(density_tiles, entry[1], entry[2], entry[3]) for entry in slots_at]
    from_left = from_behind(packed[2], "dev", 1)
    from_right = from_behind(packed[0], "dev", -1)
    stacked = jnp.stack([from_left, packed[1], from_right])
    owner_dev = own_blocks // BLK_DEV
    side_of = jnp.mod(owner_dev - own_index + 1, devices)
    same_owner = owner_dev[:, :, None] == owner_dev[:, None, :]
    earlier = jnp.arange(KB)[None, :] < jnp.arange(KB)[:, None]
    slot_rank = jnp.sum((same_owner & earlier[None, :, :]).astype(jnp.int32), axis=2)
    brick_rows = stacked[side_of, jnp.arange(bricks, dtype=jnp.int32)[:, None], slot_rank]
    block_density = brick_rows.reshape(bricks, KB * FB, KB * FB)
    applied = jnp.einsum(
        "bmn,bnc->bmc", block_density, orbitals, preferred_element_type=jnp.float32
    )
    density = jnp.sum(orbitals.astype(jnp.float32) * applied, axis=1)
    potential = hartree_exchange(density, devices)
    weighted = (orbitals.astype(jnp.float32) * potential[:, None, :]).astype(jnp.bfloat16)
    ham_brick = (
        jnp.einsum("bmc,bnc->bmn", weighted, orbitals, preferred_element_type=jnp.float32) * scale
    )
    ham_split = ham_brick.reshape(bricks, KB, FB, KB * FB)
    outgoing = []
    for holder in neighbours:
        slot_pick, row_blocks, col_blocks, is_valid = owned_slots(own_blocks, holder, devices)
        picked = jnp.take_along_axis(ham_split, slot_pick[:, :, None, None], axis=1)
        outgoing.append(picked * is_valid[:, :, None, None].astype(jnp.float32))
    back_from_right = from_behind(outgoing[0], "dev", -1)
    back_from_left = from_behind(outgoing[2], "dev", 1)
    for received, entry in (
        (back_from_left, slots_at[0]),
        (outgoing[1], slots_at[1]),
        (back_from_right, slots_at[2]),
    ):
        ham_tiles = scatter_rows(ham_tiles, received, entry[1], entry[2])
    return (potential, ham_tiles.reshape(BLK_DEV * FB, 5 * BLK_DEV * FB))


def solution(mesh):
    placed = (P("dev", None), P(), P(), P(), P(), P())
    return jax.shard_map(
        local,
        mesh=mesh,
        in_specs=placed,
        out_specs=(P("dev", None), P("dev", None)),
        check_vma=False,
    )
```

profile of v0, /device:TPU:5, one launch (start us, length us, event | category | flops | bytes accessed | tf_op | source)
XLA Modules:
  0.0 364.6 jit_solution(16645163978632066803)
XLA Ops:
  0.7 10.3 %reshape.1641 = bf16[6,128,30,128]{3,2,1,0:T(8,128)(2,1)} reshape(bf16[768,3840]{1,0:T(8,128)(2,1)} %param.14) | data formatting | bytes 11796480 | tf_op jit(solution)/shard_map/reshape | solution.py:137
  11.0 7.6 %copy.51 = bf16[6,128,30,128]{3,1,2,0:T(8,128)(2,1)} copy(bf16[6,128,30,128]{3,2,1,0:T(8,128)(2,1)} %reshape.1641) | data formatting | bytes 11796480 | tf_op jit(solution)/shard_map/reshape | solution.py:137
  19.8 0.6 gather_fusion.11
  21.1 0.6 gather_fusion.8
  22.3 5.6 %gather_fusion.12 = bf16[4,128,30,128]{3,1,2,0:T(8,128)(2,1)} fusion(bf16[6,128,30,128]{3,1,2,0:T(8,128)(2,1)} %copy.51, s32[1024]{0:T(1024)S(1)} %pad_clamp_fusion.3), kind=kCustom, calls=%fused_computation.7.clone | custom fusion | bytes 7864336 | tf_op jit(solution)/shard_map/jit(_take)/gather | solution.py:89
  28.0 4.5 %bitcast_select_fusion = bf16[1,4,128,30,128]{4,2,3,1,0:T(8,128)(2,1)} fusion(bf16[4,128,30,128]{3,1,2,0:T(8,128)(2,1)} %gather_fusion.12, pred[4]{0:T(512)(128)(4,1)S(1)} %get-tuple-element.69), kind=kLoop, calls=%fused_computation.32 | loop fusion | flops 1966080 | bytes 7864324 | tf_op jit(solution)/shard_map/jit(_take)/select_n | solution.py:89
  33.0 2.9 gather_fusion.13
  36.2 0.7 copy.56
  36.9 0.7 collective-permute-start.1
  38.2 0.6 gather_fusion.5
  38.9 5.6 %gather_fusion.6 = bf16[4,128,30,128]{3,1,2,0:T(8,128)(2,1)} fusion(bf16[6,128,30,128]{3,1,2,0:T(8,128)(2,1)} %copy.51, s32[1024]{0:T(1024)S(1)} %pad_clamp_fusion.7), kind=kCustom, calls=%fused_computation.1.clone | custom fusion | bytes 7864336 | tf_op jit(solution)/shard_map/jit(_take)/gather | solution.py:89
  45.3 4.5 %bitcast_select_fusion.2 = bf16[1,4,128,30,128]{4,2,3,1,0:T(8,128)(2,1)} fusion(bf16[4,128,30,128]{3,1,2,0:T(8,128)(2,1)} %gather_fusion.6, pred[4]{0:T(512)(128)(4,1)S(1)} %and_bitcast_fusion.5), kind=kLoop, calls=%fused_computation.34 | loop fusion | flops 1966080 | bytes 7864324 | tf_op jit(solution)/shard_map/jit(_take)/select_n | solution.py:89
  49.7 2.9 gather_fusion.7
  52.8 1.3 copy.52
  54.1 1.3 collective-permute-start
  56.3 6.2 %gather_fusion.1 = f32[1024]{0:T(1024)S(1)} fusion(f32[24576]{0:T(1024)S(1)} %copy-done, s32[1024]{0:T(1024)S(1)} %broadcast_clamp_fusion), kind=kCustom, calls=%fused_computation.13 | custom fusion | bytes 12288 | tf_op jit(solution)/shard_map/vmap()/gather | solution.py:53
  62.5 6.2 %gather_fusion = f32[1024]{0:T(1024)S(1)} fusion(f32[24576]{0:T(1024)S(1)} %copy-done.2, s32[1024]{0:T(1024)S(1)} %broadcast_clamp_fusion), kind=kCustom, calls=%fused_computation.12 | custom fusion | bytes 12288 | tf_op jit(solution)/shard_map/vmap()/gather | solution.py:52
  68.8 6.2 %gather_fusion.2 = f32[1024]{0:T(1024)S(1)} fusion(f32[24576]{0:T(1024)S(1)} %copy-done.3, s32[1024]{0:T(1024)S(1)} %broadcast_clamp_fusion), kind=kCustom, calls=%fused_computation.14 | custom fusion | bytes 12288 | tf_op jit(solution)/shard_map/vmap()/gather | solution.py:54
  75.0 6.2 %gather_fusion.3 = f32[1024]{0:T(1024)S(1)} fusion(f32[24576]{0:T(1024)S(1)} %copy-done.4, s32[1024]{0:T(1024)S(1)} %broadcast_clamp_fusion), kind=kCustom, calls=%fused_computation.15 | custom fusion | bytes 12288 | tf_op jit(solution)/shard_map/vmap()/gather | solution.py:55
  81.2 5.7 %gather_fusion.9 = bf16[4,128,30,128]{3,1,2,0:T(8,128)(2,1)} fusion(bf16[6,128,30,128]{3,1,2,0:T(8,128)(2,1)} %copy.51, s32[1024]{0:T(1024)S(1)} %pad_clamp_fusion.5), kind=kCustom, calls=%fused_computation.6.clone | custom fusion | bytes 7864336 | tf_op jit(solution)/shard_map/jit(_take)/gather | solution.py:89
  87.1 0.6 fusion.72
  88.6 6.2 %multiply_convert_fusion.1 = bf16[1024,16,16,16]{0,3,2,1:T(8,128)(2,1)} fusion(f32[1024,16]{0,1:T(8,128)S(1)} %get-tuple-element.48, f32[1024,16,16]{0,2,1:T(8,128)S(1)} %broadcast_multiply_fusion), kind=kLoop, calls=%fused_computation.25 | loop fusion | flops 8388608 | bytes 9502720 | tf_op jit(solution)/shard_map/vmap()/convert_element_type | solution.py:60
  94.7 2.3 bitcast_select_fusion.1
  97.1 2.9 gather_fusion.10
  100.2 11.3 %copy.50 = bf16[1024,4096]{1,0:T(8,128)(2,1)} copy(bf16[1024,4096]{0,1:T(8,128)(2,1)} %bitcast.258) | data formatting | bytes 16777216 | tf_op jit(solution)/shard_map/convert_element_type | solution.py:161
  111.4 1.3 copy.54
  112.8 0.6 convert_element_type.120
  113.9 0.6 pad_clamp_fusion
  115.7 2.2 pad_maximum_fusion
  117.9 2.1 gather_fusion.4
  120.0 2.9 copy.57
  122.9 14.6 %fusion.1 = (f32[]{:T(128)}, f32[4096]{0:T(1024)S(1)}) fusion(bf16[1024,4096]{1,0:T(8,128)(2,1)} %copy.50, bf16[1024,1024]{1,0:T(8,128)(2,1)S(1)} %bitcast.268, bf16[1024,4096]{0,1:T(8,128)(2,1)} %bitcast.259), kind=kOutput, calls=%fused_computation.28 | convolution fusion | flops 8606707712 | bytes 18890756 | tf_op jit(solution)/shard_map/bmn,bnc->bmc/dot_general | solution.py:158
  137.5 42.1 %psum.7 = f32[]{:T(128)} all-reduce(f32[]{:T(128)} %get-tuple-element.4), channel_id=1, replica_groups=mesh['dev'=32] {'dev'}, use_global_device_ids=true, to_apply=%region_12.16 | all-reduce | flops 1 | bytes 8 | tf_op jit(solution)/shard_map/psum | solution.py:110
  180.8 2.6 collective-permute-start.3
  184.2 2.5 collective-permute-done.2
  186.8 11.2 %bitcast_multiply_fusion = f32[1024,1024]{1,0:T(8,128)} fusion(f32[16,16,16]{2,1,0:T(8,128)S(1)} %get-tuple-element.19, f32[1024,16]{0,1:T(8,128)S(1)} %get-tuple-element.48, f32[1024,16,16]{0,2,1:T(8,128)S(1)} %copy-done.7), kind=kOutput, calls=%fused_computation.31 | convolution fusion | flops 8620343296 | bytes 5324800 | tf_op jit(solution)/shard_map/bmc,bnc->bmn/dot_general | solution.py:165
  198.0 3.0 gather_fusion.14
  201.1 1.7 fusion.6
  202.8 3.0 gather_fusion.16
  205.8 1.6 fusion.4
  207.4 0.9 collective-permute-start.5
  208.4 2.9 gather_fusion.15
  211.3 1.6 fusion.5
  212.9 2.9 copy.62
  215.9 1.9 copy.63
  217.8 4.0 %broadcast.1487.clone.1 = f32[4,128,30,128]{3,1,2,0:T(8,128)} broadcast(f32[]{:T(128)} %constant.217.clone.1), dimensions={} | broadcast | bytes 7864324 | tf_op jit(solution)/shard_map/broadcast.68
  221.9 4.4 %scatter_fusion.4 = f32[4,128,30,128]{3,1,2,0:T(8,128)} fusion(f32[4,128,30,128]{3,1,2,0:T(8,128)} %broadcast.1487.clone.1, s32[8]{0:T(128)S(1)} %copy-done.25, f32[8,4,128,128]{3,2,1,0:T(8,128)S(1)} %copy.63), kind=kCustom, calls=%fused_computation.21 | custom fusion | flops 524288 | bytes 6291488 | tf_op jit(solution)/shard_map/vmap(vmap())/scatter-add | solution.py:102
  226.3 0.7 add_subtract_fusion
  226.9 14.5 %collective-permute-done.4 = f32[1,4,128,1024]{3,2,1,0:T(8,128)} collective-permute-done((f32[1,4,128,1024]{3,2,1,0:T(8,128)}, f32[1,4,128,1024]{3,2,1,0:T(8,128)}, u32[]{:S(2)}, u32[]{:S(2)}) %collective-permute-start.4) | collective-permute-done | bytes 2097184 | tf_op jit(solution)/shard_map/ppermute | solution.py:40
  241.4 1.9 copy.60
  243.3 1.8 copy.61
  245.1 8.9 %collective-permute-done.5 = f32[1,4,128,1024]{3,2,1,0:T(8,128)} collective-permute-done((f32[1,4,128,1024]{3,2,1,0:T(8,128)}, f32[1,4,128,1024]{3,2,1,0:T(8,128)}, u32[]{:S(2)}, u32[]{:S(2)}) %collective-permute-start.5) | collective-permute-done | bytes 2097184 | tf_op jit(solution)/shard_map/ppermute | solution.py:40
  254.0 2.9 copy.64
  256.9 1.9 copy.65
  258.9 4.1 %broadcast.1487.clone = f32[4,128,30,128]{3,1,2,0:T(8,128)} broadcast(f32[]{:T(128)} %constant.217.clone.1), dimensions={} | broadcast | bytes 7864324 | tf_op jit(solution)/shard_map/broadcast.68
  263.0 5.1 %scatter_fusion.3 = f32[4,128,30,128]{3,1,2,0:T(8,128)} fusion(f32[4,128,30,128]{3,1,2,0:T(8,128)} %broadcast.1487.clone, s32[8]{0:T(128)S(1)} %copy-done.24, f32[8,4,128,128]{3,2,1,0:T(8,128)} %copy.61), kind=kCustom, calls=%fused_computation.20 | custom fusion | flops 524288 | bytes 6291488 | tf_op jit(solution)/shard_map/vmap(vmap())/scatter-add | solution.py:102
  268.1 6.0 %broadcast_in_dim.67 = f32[6,128,30,128]{3,1,2,0:T(8,128)} broadcast(f32[]{:T(128)} %constant.217.clone.1), dimensions={} | broadcast | bytes 11796484 | tf_op jit(solution)/shard_map/broadcast_in_dim | solution.py:144
  274.2 15.0 %scatter_fusion = f32[6,128,30,128]{3,1,2,0:T(8,128)} fusion(f32[6,128,30,128]{3,1,2,0:T(8,128)} %broadcast_in_dim.67, s32[4]{0:T(128)S(1)} %copy-done.18, f32[4,128,30,128]{3,1,2,0:T(8,128)} %scatter_fusion.3), kind=kCustom, calls=%fused_computation.17 | custom fusion | flops 1966080 | bytes 23592976 | tf_op jit(solution)/shard_map/scatter-add | solution.py:105
  289.1 15.0 %scatter_fusion.1 = f32[6,128,30,128]{3,1,2,0:T(8,128)} fusion(f32[6,128,30,128]{3,1,2,0:T(8,128)} %scatter_fusion, s32[4]{0:T(128)S(1)} %copy-done.16, f32[4,128,30,128]{3,1,2,0:T(8,128)} %scatter_fusion.4), kind=kCustom, calls=%fused_computation.18 | custom fusion | flops 1966080 | bytes 23592976 | tf_op jit(solution)/shard_map/scatter-add | solution.py:105
  304.1 4.1 %broadcast.1487.clone.2 = f32[4,128,30,128]{3,1,2,0:T(8,128)} broadcast(f32[]{:T(128)} %constant.217.clone.1), dimensions={} | broadcast | bytes 7864324 | tf_op jit(solution)/shard_map/broadcast.68
  308.2 4.4 %scatter_fusion.5 = f32[4,128,30,128]{3,1,2,0:T(8,128)} fusion(f32[4,128,30,128]{3,1,2,0:T(8,128)} %broadcast.1487.clone.2, s32[8]{0:T(128)S(1)} %copy-done.21, f32[8,4,128,128]{3,2,1,0:T(8,128)S(1)} %copy.65), kind=kCustom, calls=%fused_computation.22 | custom fusion | flops 524288 | bytes 6291488 | tf_op jit(solution)/shard_map/vmap(vmap())/scatter-add | solution.py:102
  312.6 15.1 %scatter_fusion.2 = f32[6,128,30,128]{3,1,2,0:T(8,128)} fusion(f32[6,128,30,128]{3,1,2,0:T(8,128)} %scatter_fusion.1, s32[4]{0:T(128)S(1)} %copy-done.20, f32[4,128,30,128]{3,1,2,0:T(8,128)} %scatter_fusion.5), kind=kCustom, calls=%fused_computation.19 | custom fusion | flops 1966080 | bytes 23592976 | tf_op jit(solution)/shard_map/scatter-add | solution.py:105
  327.7 15.7 %copy.66 = f32[6,128,30,128]{3,2,1,0:T(8,128)} copy(f32[6,128,30,128]{3,1,2,0:T(8,128)} %scatter_fusion.2) | data formatting | bytes 23592960 | tf_op jit(solution)/shard_map/scatter-add | solution.py:105
  343.4 21.0 %copy.70 = f32[96,8,30,128]{3,1,2,0:T(8,128)} copy(f32[96,8,30,128]{3,2,1,0:T(8,128)} %bitcast.257) | data formatting | bytes 23592960
  (153 shorter events, 10.3 us)
Async XLA Ops:
  0.6 55.7 %copy-start = (f32[24576]{0:T(1024)S(1)}, f32[24576]{0:T(1024)}, u32[]{:S(2)}) copy-start(f32[24576]{0:T(1024)} %param.15) | copy-start | bytes 294916
  11.0 7.6 %copy-start.10 = (s32[32,8]{0,1:T(8,128)S(1)}, s32[32,8]{0,1:T(8,128)}, u32[]{:S(2)}) copy-start(s32[32,8]{0,1:T(8,128)} %param.19) | copy-start | bytes 3076
  20.4 0.5 copy-start.17
  36.9 78.8 %collective-permute-start.1 = (bf16[1,4,128,1024]{2,3,1,0:T(8,128)(2,1)S(1)}, bf16[1,4,128,1024]{2,3,1,0:T(8,128)(2,1)}, u32[]{:S(2)}, u32[]{:S(2)}) collective-permute-start(bf16[1,4,128,1024]{2,3,1,0:T(8,128)(2,1)S(1)} %bitcast.269), channel_id=1, source_target_pairs={{0,31},{1,0},{2,1},{3,2},{4,3},{5,4},{6,5},{7,6},{8,7},{9,8},{10,9... | collective-permute-start | bytes 3145736 | tf_op jit(solution)/shard_map/ppermute | solution.py:40
  38.2 61.8 %copy-start.27 = (pred[4]{0:T(512)(128)(4,1)}, pred[4]{0:T(512)(128)(4,1)S(1)}, u32[]{:S(2)}) copy-start(pred[4]{0:T(512)(128)(4,1)S(1)} %get-tuple-element.79) | copy-start | bytes 16
  38.2 42.9 %copy-start.15 = (s32[4]{0:T(128)}, s32[4]{0:T(128)S(1)}, u32[]{:S(2)}) copy-start(s32[4]{0:T(128)S(1)} %get-tuple-element.74) | copy-start | bytes 52
  38.9 5.7 %copy-start.19 = (s32[4]{0:T(128)}, s32[4]{0:T(128)S(1)}, u32[]{:S(2)}) copy-start(s32[4]{0:T(128)S(1)} %fusion.75) | copy-start | bytes 52
  52.6 9.9 %copy-start.2 = (f32[24576]{0:T(1024)S(1)}, f32[24576]{0:T(1024)}, u32[]{:S(2)}) copy-start(f32[24576]{0:T(1024)} %param.18) | copy-start | bytes 294916
  54.1 61.6 %collective-permute-start = (bf16[1,4,128,1024]{2,3,1,0:T(8,128)(2,1)}, bf16[1,4,128,1024]{2,3,1,0:T(8,128)(2,1)}, u32[]{:S(2)}, u32[]{:S(2)}) collective-permute-start(bf16[1,4,128,1024]{2,3,1,0:T(8,128)(2,1)} %bitcast.17), channel_id=1, source_target_pairs={{0,1},{1,2},{2,3},{3,4},{4,5},{5,6},{6,7},{7,8},{8,9},{9,10},{10,1... | collective-permute-start | bytes 3145736 | tf_op jit(solution)/shard_map/ppermute | solution.py:40
  56.3 12.5 %copy-start.3 = (f32[24576]{0:T(1024)S(1)}, f32[24576]{0:T(1024)}, u32[]{:S(2)}) copy-start(f32[24576]{0:T(1024)} %param.16) | copy-start | bytes 294916
  62.5 12.5 %copy-start.4 = (f32[24576]{0:T(1024)S(1)}, f32[24576]{0:T(1024)}, u32[]{:S(2)}) copy-start(f32[24576]{0:T(1024)} %param.17) | copy-start | bytes 294916
  88.6 6.2 %copy-start.6 = (f32[1024,16,16]{0,2,1:T(8,128)}, f32[1024,16,16]{0,2,1:T(8,128)S(1)}, u32[]{:S(2)}) copy-start(f32[1024,16,16]{0,2,1:T(8,128)S(1)} %broadcast_multiply_fusion) | copy-start | bytes 3145732
  88.6 6.2 %copy-start.5 = (bf16[4,128,30,128]{3,1,2,0:T(8,128)(2,1)S(1)}, bf16[4,128,30,128]{3,1,2,0:T(8,128)(2,1)}, u32[]{:S(2)}) copy-start(bf16[4,128,30,128]{3,1,2,0:T(8,128)(2,1)} %gather_fusion.9) | copy-start | bytes 11796484
  137.5 49.3 %copy-start.7 = (f32[1024,16,16]{0,2,1:T(8,128)S(1)}, f32[1024,16,16]{0,2,1:T(8,128)}, u32[]{:S(2)}) copy-start(f32[1024,16,16]{0,2,1:T(8,128)} %copy-done.6) | copy-start | bytes 3145732
  180.3 3.4 copy-start.13
  180.3 17.7 %copy-start.8 = (f32[4096]{0:T(1024)}, f32[4096]{0:T(1024)S(1)}, u32[]{:S(2)}) copy-start(f32[4096]{0:T(1024)S(1)} %get-tuple-element.45) | copy-start | bytes 49156
  180.3 17.7 %copy-start.11 = (f32[4096]{0:T(1024)}, f32[4096]{0:T(1024)S(1)}, u32[]{:S(2)}) copy-start(f32[4096]{0:T(1024)S(1)} %get-tuple-element.43) | copy-start | bytes 49156
  180.8 3.4 collective-permute-start.3
  183.4 3.3 collective-permute-start.2
  198.0 3.0 copy-start.30
  198.0 3.0 copy-start.31
  201.0 4.7 %copy-start.23 = (pred[4]{0:T(512)(128)(4,1)S(1)}, pred[4]{0:T(512)(128)(4,1)}, u32[]{:S(2)}) copy-start(pred[4]{0:T(512)(128)(4,1)} %get-tuple-element.67) | copy-start | bytes 16
  201.0 4.7 %copy-start.29 = (f32[4]{0:T(128)S(1)}, f32[4]{0:T(128)}, u32[]{:S(2)}) copy-start(f32[4]{0:T(128)} %convert_element_type.123) | copy-start | bytes 52
  202.7 5.6 %copy-start.28 = (pred[4]{0:T(512)(128)(4,1)S(1)}, pred[4]{0:T(512)(128)(4,1)}, u32[]{:S(2)}) copy-start(pred[4]{0:T(512)(128)(4,1)} %copy-done.27) | copy-start | bytes 16
  202.7 5.6 %copy-start.26 = (s32[4]{0:T(128)S(1)}, s32[4]{0:T(128)}, u32[]{:S(2)}) copy-start(s32[4]{0:T(128)} %get-tuple-element.76) | copy-start | bytes 52
  202.7 38.6 %collective-permute-start.4 = (f32[1,4,128,1024]{3,2,1,0:T(8,128)}, f32[1,4,128,1024]{3,2,1,0:T(8,128)}, u32[]{:S(2)}, u32[]{:S(2)}) collective-permute-start(f32[1,4,128,1024]{3,2,1,0:T(8,128)} %fusion.6), channel_id=1, source_target_pairs={{0,1},{1,2},{2,3},{3,4},{4,5},{5,6},{6,7},{7,8},{8,9},{9,10},{10,1... | collective-permute-start | bytes 6291464 | tf_op jit(solution)/shard_map/ppermute | solution.py:40
  205.8 5.5 %copy-start.22 = (pred[4]{0:T(512)(128)(4,1)S(1)}, pred[4]{0:T(512)(128)(4,1)}, u32[]{:S(2)}) copy-start(pred[4]{0:T(512)(128)(4,1)} %get-tuple-element.68) | copy-start | bytes 16
  207.4 46.6 %collective-permute-start.5 = (f32[1,4,128,1024]{3,2,1,0:T(8,128)}, f32[1,4,128,1024]{3,2,1,0:T(8,128)}, u32[]{:S(2)}, u32[]{:S(2)}) collective-permute-start(f32[1,4,128,1024]{3,2,1,0:T(8,128)} %fusion.4), channel_id=1, source_target_pairs={{0,31},{1,0},{2,1},{3,2},{4,3},{5,4},{6,5},{7,6},{8,7},{9,8},{10,9... | collective-permute-start | bytes 6291464 | tf_op jit(solution)/shard_map/ppermute | solution.py:40
  217.8 4.1 %copy-start.25 = (s32[8]{0:T(128)S(1)}, s32[8]{0:T(128)}, u32[]{:S(2)}) copy-start(s32[8]{0:T(128)} %get-tuple-element.72) | copy-start | bytes 100
  221.8 4.4 %copy-start.9 = (f32[4096]{0:T(1024)S(1)}, f32[4096]{0:T(1024)}, u32[]{:S(2)}) copy-start(f32[4096]{0:T(1024)} %copy-done.8) | copy-start | bytes 49156
  221.8 4.4 %copy-start.12 = (f32[4096]{0:T(1024)S(1)}, f32[4096]{0:T(1024)}, u32[]{:S(2)}) copy-start(f32[4096]{0:T(1024)} %copy-done.11) | copy-start | bytes 49156
  221.9 4.4 %copy-start.14 = (f32[4096]{0:T(1024)S(1)}, f32[4096]{0:T(1024)}, u32[]{:S(2)}) copy-start(f32[4096]{0:T(1024)} %copy-done.13) | copy-start | bytes 49156
  258.9 4.1 %copy-start.24 = (s32[8]{0:T(128)S(1)}, s32[8]{0:T(128)}, u32[]{:S(2)}) copy-start(s32[8]{0:T(128)} %get-tuple-element.65) | copy-start | bytes 100
  268.1 6.0 %copy-start.18 = (s32[4]{0:T(128)S(1)}, s32[4]{0:T(128)}, u32[]{:S(2)}) copy-start(s32[4]{0:T(128)} %copy-done.17) | copy-start | bytes 52
  274.2 15.0 %copy-start.16 = (s32[4]{0:T(128)S(1)}, s32[4]{0:T(128)}, u32[]{:S(2)}) copy-start(s32[4]{0:T(128)} %copy-done.15) | copy-start | bytes 52
  304.1 4.1 %copy-start.21 = (s32[8]{0:T(128)S(1)}, s32[8]{0:T(128)}, u32[]{:S(2)}) copy-start(s32[8]{0:T(128)} %get-tuple-element.61) | copy-start | bytes 100
  308.2 4.4 %copy-start.20 = (s32[4]{0:T(128)S(1)}, s32[4]{0:T(128)}, u32[]{:S(2)}) copy-start(s32[4]{0:T(128)} %copy-done.19) | copy-start | bytes 52
  343.4 21.0 %copy-start.1 = (f32[24576]{0:T(1024)S(1)}, f32[24576]{0:T(1024)}, u32[]{:S(2)}) copy-start(f32[24576]{0:T(1024)} %param.15) | copy-start | bytes 294916
where the time goes:
time: 372 us; the launch traced here: 365 us
  local copies, waits for them, and re-layouts  168 us (45%)
  other arithmetic  94.6 us (25%)
  blocking collectives  42.1 us (11%)
  waiting for transfers between devices  26.2 us (7%)
  matrix products  25.8 us (7%)
  starting transfers between devices  5.68 us (2%)
    scatter-add x3, other arithmetic, scatter_rows(): return ham_tiles.at[row_blocks].add(widened)  45 us
    psum x1, blocking collectives, hartree_exchange(): charge = lax.psum(jnp.sum(density), 'dev')  42.1 us
    ppermute x4, waiting for transfers between devices, from_behind(): return lax.ppermute(value, axis, pairs)  23.4 us
    unnamed x65, local copies, waits for them, and re-layouts  21.3 us
    reshape x2, local copies, waits for them, and re-layouts, local(): density_tiles = density_rows.reshape(BLK_DEV, FB, 5 * BLK_DEV, FB)  17.9 us
    gather x3, local copies, waits for them, and re-layouts, pack_rows(): full_rows = jnp.take(density_tiles, row_blocks, axis=0)  17 us
    scatter-add x1, local copies, waits for them, and re-layouts, scatter_rows(): return ham_tiles.at[row_blocks].add(widened)  15.7 us
    scatter-add x5, other arithmetic, spread(): jnp.zeros((FB, 5 * BLK_DEV, FB), jnp.float32).at[:, cols_one, :].add(piece)  15 us
  transfers between devices with their start and end apart: 6, of which 4 were waited for; matrix products, arithmetic and copies ran while one was open for 28% of the time, Pallas kernels for 0%

commit v1 on v0

v1 whole, which is shorter than its diff:
```python
import functools
import math

import jax
import jax.numpy as jnp
from jax import lax
from jax.experimental import pallas as pl
from jax.experimental.pallas import tpu as pltpu
from jax.sharding import PartitionSpec as P

FB = 128
KB = 8
CAP = 4
BLK_DEV = 6
SIDE = 16
LAYER = SIDE * SIDE
CELLS = SIDE * SIDE * SIDE
COLS = 5 * BLK_DEV * FB
ROWS = BLK_DEV * FB
HALF = 64
VMEM_BYTES = 60 * 1024 * 1024

omega = 2.0 / 3.0
four_pi = 4.0 * math.pi
slater = (3.0 / math.pi) ** (1.0 / 3.0)
f32 = jnp.float32
bf16 = jnp.bfloat16


def wrapped(distance):
    moved = distance + 0.5
    return (moved - jnp.floor(moved)) - 0.5


def fill_orbitals(brick, devices, bb_ref, param_refs, rows_ref, orb_ref):
    point = (lax.broadcasted_iota(jnp.int32, (HALF, SIDE), 1).astype(f32) + 0.5) / SIDE
    cell = lax.broadcasted_iota(jnp.int32, (HALF, LAYER), 1)
    point_y = ((cell // SIDE).astype(f32) + 0.5) / SIDE
    point_z = ((cell % SIDE).astype(f32) + 0.5) / SIDE

    def one_block(a, carry):
        block = bb_ref[brick, a]
        owner = block // BLK_DEV
        offset = (lax.rem(brick - owner + 1 + devices, devices) - 1).astype(f32)
        for p, ref in enumerate(param_refs):
            rows_ref[p : p + 1, :] = ref[pl.ds(block, 1), :]
        turned = rows_ref[...].T
        for h in range(FB // HALF):
            part = turned[h * HALF : (h + 1) * HALF]
            rate = -part[:, 3:4]
            along_x = (offset + point) - part[:, 0:1]
            along_y = wrapped(point_y - part[:, 1:2])
            along_z = wrapped(point_z - part[:, 2:3])
            factor_x = jnp.exp(rate * along_x * along_x)
            factor_yz = jnp.exp(rate * along_y * along_y) * jnp.exp(rate * along_z * along_z)
            start = pl.multiple_of(a * FB + h * HALF, HALF)
            for i in range(SIDE):
                orb_ref[pl.ds(start, HALF), i * LAYER : (i + 1) * LAYER] = (
                    factor_x[:, i : i + 1] * factor_yz
                ).astype(bf16)
        return carry

    lax.fori_loop(0, KB, one_block, 0)


def find_slots(brick, me, bb_ref, sel_ref):
    for k in range(CAP):
        sel_ref[k] = 0
    count = jnp.int32(0)
    for a in range(KB):
        mine = bb_ref[brick, a] // BLK_DEV == me

        @pl.when(mine)
        def _():
            sel_ref[count] = a

        count = count + mine.astype(jnp.int32)
    return count


def column_block(brick, c, me, devices, bb_ref):
    block = bb_ref[brick, c]
    owner = block // BLK_DEV
    return lax.rem(owner - me + 2 + devices, devices) * BLK_DEV + (block - owner * BLK_DEV)


def row_block(brick, slot, bb_ref):
    return lax.rem(bb_ref[brick, slot], BLK_DEV)


def density_kernel(
    devices, bb_ref, rows_hbm, cx, cy, cz, ex, pd_ref, sum_ref, rows_vmem, orb_ref, mat_ref, tmp_ref, sel_ref, sem
):
    me = lax.axis_index("dev")
    load = pltpu.make_async_copy(rows_hbm, rows_vmem, sem)
    load.start()
    tmp_ref[...] = jnp.zeros_like(tmp_ref)

    def one_brick(t, carry):
        brick = lax.rem(me + t - 1 + devices, devices)
        fill_orbitals(brick, devices, bb_ref, (cx, cy, cz, ex), tmp_ref, orb_ref)
        count = find_slots(brick, me, bb_ref, sel_ref)

        @pl.when(t == 0)
        def _():
            load.wait()

        for k in range(CAP):
            here = pl.ds(k * FB, FB)

            @pl.when(k < count)
            def _():
                row = pl.multiple_of(row_block(brick, sel_ref[k], bb_ref) * FB, FB)
                for c in range(KB):
                    col = pl.multiple_of(column_block(brick, c, me, devices, bb_ref) * FB, FB)
                    mat_ref[here, c * FB : (c + 1) * FB] = rows_vmem[pl.ds(row, FB), pl.ds(col, FB)]

            @pl.when(k >= count)
            def _():
                mat_ref[here, :] = jnp.zeros((FB, KB * FB), bf16)

        def one_chunk(j, inner):
            chunk = pl.ds(pl.multiple_of(j * 2 * LAYER, 2 * LAYER), 2 * LAYER)
            applied = jnp.dot(mat_ref[...], orb_ref[:, chunk], preferred_element_type=f32)
            total = jnp.zeros((1, 2 * LAYER), f32)
            for k in range(CAP):
                row = pl.multiple_of(sel_ref[k] * FB, FB)
                own = orb_ref[pl.ds(row, FB), chunk].astype(f32)
                total = total + jnp.sum(own * applied[k * FB : (k + 1) * FB], axis=0, keepdims=True)
            pd_ref[t, pl.ds(2 * j, 1), :] = total[:, :LAYER]
            pd_ref[t, pl.ds(2 * j + 1, 1), :] = total[:, LAYER:]
            return inner

        lax.fori_loop(0, SIDE // 2, one_chunk, 0)
        return carry

    lax.fori_loop(0, 3, one_brick, 0)
    layer = jnp.sum(pd_ref[0] + pd_ref[1] + pd_ref[2], axis=0, keepdims=True)
    sum_ref[0] = layer[:, :FB] + layer[:, FB:]


def potential_kernel(
    devices, pd_ref, sum_ref, out_ref, left1, right1, left2, right2, left3, right3, sums, send_sem, recv_sem, all_sem
):
    me = lax.axis_index("dev")
    barrier = pltpu.get_barrier_semaphore()

    def at(step):
        return lax.rem(me + step + devices, devices)

    def greet(k, carry):
        pl.semaphore_signal(
            barrier, inc=1, device_id=(lax.rem(me + k, devices),), device_id_type=pl.DeviceIdType.MESH
        )
        return carry

    lax.fori_loop(1, devices, greet, 0)
    pl.semaphore_wait(barrier, devices - 1)

    def to_all(k):
        return pltpu.make_async_remote_copy(
            src_ref=sum_ref.at[0],
            dst_ref=sums.at[k - 1],
            send_sem=all_sem.at[0],
            recv_sem=all_sem.at[1],
            device_id=(lax.rem(me + k, devices),),
            device_id_type=pl.DeviceIdType.MESH,
        )

    def start_sum(k, carry):
        to_all(k).start()
        return carry

    plan = (
        (pd_ref, left1, 1),
        (pd_ref, right1, -1),
        (pd_ref.at[pl.ds(1, 2)], left2, 2),
        (pd_ref.at[pl.ds(0, 2)], right2, -2),
        (pd_ref.at[2, pl.ds(8, 8)], left3, 3),
        (pd_ref.at[0, pl.ds(0, 8)], right3, -3),
    )
    copies = [
        pltpu.make_async_remote_copy(
            src_ref=src,
            dst_ref=dst,
            send_sem=send_sem.at[q],
            recv_sem=recv_sem.at[q],
            device_id=(at(step),),
            device_id_type=pl.DeviceIdType.MESH,
        )
        for q, (src, dst, step) in enumerate(plan)
    ]
    lax.fori_loop(1, devices, start_sum, 0)
    for copy in copies:
        copy.start()
    for copy in copies:
        copy.wait()
    pltpu.make_async_copy(sums, sums, all_sem.at[0]).wait()
    pltpu.make_async_copy(sums, sums, all_sem.at[1]).wait()

    total = jnp.sum(sums[...], axis=0) + sum_ref[0]
    average = jnp.sum(total, axis=1, keepdims=True) / (devices * CELLS)
    scale = omega * four_pi / 6.0
    here = pd_ref[1] + left1[2] + right1[0]
    behind = left1[1] + left2[1] + pd_ref[0]
    ahead = right1[1] + right2[0] + pd_ref[2]
    far_behind = (left2[0, 8:] + left3[...] + left1[0, 8:])[7:]
    far_ahead = (right2[1, :8] + right3[...] + right1[2, :8])[:1]
    lane = lax.broadcasted_iota(jnp.int32, (SIDE, LAYER), 1) % SIDE
    row = lax.broadcasted_iota(jnp.int32, (SIDE, LAYER), 0)
    cases = (
        (behind, far_behind, here[:1]),
        (here, behind[SIDE - 1 :], ahead[:1]),
        (ahead, here[SIDE - 1 :], far_ahead),
    )

    def moved(x, steps, axis):
        return pltpu.roll(x, steps % x.shape[axis], axis)

    for t, (density, before, after) in enumerate(cases):
        source = density - average
        one = scale * source
        up = jnp.where(row == 0, scale * (before - average), moved(one, 1, 0))
        down = jnp.where(row == SIDE - 1, scale * (after - average), moved(one, -1, 0))
        beside = up + down + moved(one, SIDE, 1) + moved(one, -SIDE, 1)
        beside = beside + jnp.where(lane == 0, moved(one, 1 - SIDE, 1), moved(one, 1, 1))
        beside = beside + jnp.where(lane == SIDE - 1, moved(one, SIDE - 1, 1), moved(one, -1, 1))
        two = one + omega * ((four_pi * source + beside) / 6.0 - one)
        size = jnp.abs(density)
        safe = jnp.where(size > 0.0, size, 1.0)
        root = jnp.exp(jnp.log(safe) / 3.0)
        root = root - (root - safe / (root * root)) / 3.0
        root = jnp.where(size > 0.0, root, 0.0)
        root = jnp.where(density < 0.0, -root, root)
        out_ref[t] = two - slater * root


def ham_kernel(devices, bb_ref, pot_ref, cx, cy, cz, ex, out_hbm, acc_ref, orb_ref, wei_ref, tmp_ref, sel_ref, sem):
    me = lax.axis_index("dev")
    tmp_ref[...] = jnp.zeros_like(tmp_ref)

    def clear(r, carry):
        acc_ref[pl.ds(pl.multiple_of(r * 64, 64), 64), :] = jnp.zeros((64, COLS), f32)
        return carry

    lax.fori_loop(0, ROWS // 64, clear, 0)

    def one_brick(t, carry):
        brick = lax.rem(me + t - 1 + devices, devices)
        fill_orbitals(brick, devices, bb_ref, (cx, cy, cz, ex), tmp_ref, orb_ref)
        count = find_slots(brick, me, bb_ref, sel_ref)

        def weigh(k, inner):
            source = pl.multiple_of(sel_ref[k] * FB, FB)
            target = pl.multiple_of(k * FB, FB)
            for i in range(SIDE):
                cells = slice(i * LAYER, (i + 1) * LAYER)
                wei_ref[pl.ds(target, FB), cells] = (
                    orb_ref[pl.ds(source, FB), cells].astype(f32) * pot_ref[t, i : i + 1, :]
                ).astype(bf16)
            return inner

        lax.fori_loop(0, CAP, weigh, 0)

        def one_pair(q, inner):
            part = orb_ref[pl.ds(pl.multiple_of(q * 2 * FB, 2 * FB), 2 * FB), :]
            tile = lax.dot_general(
                wei_ref[...], part, (((1,), (1,)), ((), ())), preferred_element_type=f32
            ) * (64.0 / CELLS)
            for k in range(CAP):

                @pl.when(k < count)
                def _():
                    row = pl.multiple_of(row_block(brick, sel_ref[k], bb_ref) * FB, FB)
                    for c in range(2):
                        col = pl.multiple_of(column_block(brick, 2 * q + c, me, devices, bb_ref) * FB, FB)
                        acc_ref[pl.ds(row, FB), pl.ds(col, FB)] += tile[
                            k * FB : (k + 1) * FB, c * FB : (c + 1) * FB
                        ]

            return inner

        lax.fori_loop(0, KB // 2, one_pair, 0)
        return carry

    lax.fori_loop(0, 3, one_brick, 0)
    store = pltpu.make_async_copy(acc_ref, out_hbm, sem)
    store.start()
    store.wait()


def local(devices, density_rows, center_x, center_y, center_z, exponent, brick_blocks):
    params = [x.reshape(-1, FB) for x in (center_x, center_y, center_z, exponent)]
    vmem = pl.BlockSpec(memory_space=pltpu.VMEM)
    smem = pl.BlockSpec(memory_space=pltpu.SMEM)
    anywhere = pl.BlockSpec(memory_space=pl.ANY)
    grid = (3, SIDE, LAYER)
    partial, sums = pl.pallas_call(
        functools.partial(density_kernel, devices),
        out_shape=(jax.ShapeDtypeStruct(grid, f32), jax.ShapeDtypeStruct((1, 1, FB), f32)),
        in_specs=[smem, anywhere] + [vmem] * 4,
        out_specs=(vmem, vmem),
        scratch_shapes=[
            pltpu.VMEM((ROWS, COLS), bf16),
            pltpu.VMEM((KB * FB, CELLS), bf16),
            pltpu.VMEM((CAP * FB, KB * FB), bf16),
            pltpu.VMEM((8, FB), f32),
            pltpu.SMEM((CAP,), jnp.int32),
            pltpu.SemaphoreType.DMA,
        ],
        compiler_params=pltpu.CompilerParams(vmem_limit_bytes=VMEM_BYTES),
        name="partial_density",
    )(brick_blocks, density_rows, *params)
    potentials = pl.pallas_call(
        functools.partial(potential_kernel, devices),
        out_shape=jax.ShapeDtypeStruct(grid, f32),
        in_specs=[vmem, vmem],
        out_specs=vmem,
        scratch_shapes=[
            pltpu.VMEM((3, SIDE, LAYER), f32),
            pltpu.VMEM((3, SIDE, LAYER), f32),
            pltpu.VMEM((2, SIDE, LAYER), f32),
            pltpu.VMEM((2, SIDE, LAYER), f32),
            pltpu.VMEM((8, LAYER), f32),
            pltpu.VMEM((8, LAYER), f32),
            pltpu.VMEM((devices - 1, 1, FB), f32),
            pltpu.SemaphoreType.DMA((6,)),
            pltpu.SemaphoreType.DMA((6,)),
            pltpu.SemaphoreType.DMA((2,)),
        ],
        compiler_params=pltpu.CompilerParams(collective_id=0, has_side_effects=True),
        name="exchange_potential",
    )(partial, sums)
    ham = pl.pallas_call(
        functools.partial(ham_kernel, devices),
        out_shape=jax.ShapeDtypeStruct((ROWS, COLS), f32),
        in_specs=[smem] + [vmem] * 5,
        out_specs=anywhere,
        scratch_shapes=[
            pltpu.VMEM((ROWS, COLS), f32),
            pltpu.VMEM((KB * FB, CELLS), bf16),
            pltpu.VMEM((CAP * FB, CELLS), bf16),
            pltpu.VMEM((8, FB), f32),
            pltpu.SMEM((CAP,), jnp.int32),
            pltpu.SemaphoreType.DMA,
        ],
        compiler_params=pltpu.CompilerParams(vmem_limit_bytes=VMEM_BYTES),
        name="ham_rows",
    )(brick_blocks, potentials, *params)
    return potentials[1].reshape(1, CELLS), ham


def solution(mesh):
    placed = (P("dev", None), P(), P(), P(), P(), P())
    return jax.shard_map(
        functools.partial(local, mesh.shape["dev"]),
        mesh=mesh,
        in_specs=placed,
        out_specs=(P("dev", None), P("dev", None)),
        check_vma=False,
    )
```

time: 372 us -> 100 us (0.27)
  the two profiles are of different devices: /device:TPU:5 before, /device:TPU:0 now
where the time goes in v1:
time: 100 us; the launch traced here: 99.4 us
  Pallas kernels  96.1 us (96%)
  local copies, waits for them, and re-layouts  2.71 us (3%)
    pallas_call x1, Pallas kernels, local(): pl.pallas_call(functools.partial(ham_kernel, devices), out_shape=jax.Shap...  43.9 us
    pallas_call x1, Pallas kernels, local(): pl.pallas_call(functools.partial(density_kernel, devices), out_shape=(jax...  39 us
    pallas_call x1, Pallas kernels, local(): pl.pallas_call(functools.partial(potential_kernel, devices), out_shape=ja...  13.1 us
    unnamed x3, local copies, waits for them, and re-layouts  2.71 us

profile of v1, /device:TPU:0, one launch (start us, length us, event | category | flops | bytes accessed | tf_op | source)
XLA Modules:
  0.0 99.4 jit_solution(1501762477856259871)
XLA Ops:
  0.6 1.4 %copy.8.bb_ref = s32[32,8]{1,0:T(8,128)} copy(s32[32,8]{0,1:T(8,128)} %param.11) | data formatting | bytes 2048 | tf_op args[5]
  2.0 39.0 %partial_density.1 = (f32[3,16,256]{2,1,0:T(8,128)}, f32[1,1,128]{2,1,0:T(1,128)}) custom-call(s32[32,8]{1,0:T(8,128)} %copy.8.bb_ref, bf16[768,3840]{1,0:T(8,128)(2,1)} %rows_hbm.1, f32[192,128]{1,0:T(8,128)} %bitcast.7, f32[192,128]{1,0:T(8,128)} %bitcast.9, f32[192,128]{1,0:T(8,128)} %bitcast.11, f32[192,128]{1,0:T(8,128)} %bitcast.13), custom_call_target="tpu_custom_call" | custom-call | tf_op jit(solution)/shard_map/partial_density/pallas_call | solution.py:298
  41.0 13.1 %exchange_potential.1.pot_ref = f32[3,16,256]{2,1,0:T(8,128)} custom-call(f32[3,16,256]{2,1,0:T(8,128)} %get-tuple-element.4.pd_ref, f32[1,1,128]{2,1,0:T(1,128)} %get-tuple-element.5.sum_ref), custom_call_target="tpu_custom_call" | custom-call | tf_op jit(solution)/shard_map/exchange_potential/pallas_call | solution.py:314
  54.2 43.9 %ham_rows.1 = f32[768,3840]{1,0:T(8,128)} custom-call(s32[32,8]{1,0:T(8,128)} %copy.8.bb_ref, f32[3,16,256]{2,1,0:T(8,128)} %exchange_potential.1.pot_ref, f32[192,128]{1,0:T(8,128)} %bitcast.8, f32[192,128]{1,0:T(8,128)} %bitcast.10, f32[192,128]{1,0:T(8,128)} %bitcast.12, f32[192,128]{1,0:T(8,128)} %bitcast.14), custom_call_target="tpu_custom_call" | custom-call | tf_op jit(solution)/shard_map/ham_rows/pallas_call | solution.py:334
  98.1 0.7 slice_bitcast_fusion
  98.8 0.6 copy.10

commit v2 on v1

--- a/solution.py
+++ b/solution.py
@@ -33,30 +33,29 @@
 
 
 def fill_orbitals(brick, devices, bb_ref, param_refs, rows_ref, orb_ref):
-    point = (lax.broadcasted_iota(jnp.int32, (HALF, SIDE), 1).astype(f32) + 0.5) / SIDE
-    cell = lax.broadcasted_iota(jnp.int32, (HALF, LAYER), 1)
-    point_y = ((cell // SIDE).astype(f32) + 0.5) / SIDE
-    point_z = ((cell % SIDE).astype(f32) + 0.5) / SIDE
+    point = (lax.broadcasted_iota(jnp.int32, (SIDE, FB), 0).astype(f32) + 0.5) / SIDE
 
     def one_block(a, carry):
         block = bb_ref[brick, a]
         owner = block // BLK_DEV
         offset = (lax.rem(brick - owner + 1 + devices, devices) - 1).astype(f32)
-        for p, ref in enumerate(param_refs):
-            rows_ref[p : p + 1, :] = ref[pl.ds(block, 1), :]
-        turned = rows_ref[...].T
+        mid_x, mid_y, mid_z, rate = [ref[pl.ds(block, 1), :] for ref in param_refs]
+        rate = -rate
+        along_x = (offset + point) - mid_x
+        along_y = wrapped(point - mid_y)
+        along_z = wrapped(point - mid_z)
+        factor_x = jnp.exp(rate * along_x * along_x).T
+        factor_y = jnp.exp(rate * along_y * along_y)
+        factor_z = jnp.exp(rate * along_z * along_z)
+        for j in range(SIDE):
+            rows_ref[j * SIDE : (j + 1) * SIDE, :] = factor_y[j : j + 1] * factor_z
+        factor_yz = rows_ref[...].T
         for h in range(FB // HALF):
-            part = turned[h * HALF : (h + 1) * HALF]
-            rate = -part[:, 3:4]
-            along_x = (offset + point) - part[:, 0:1]
-            along_y = wrapped(point_y - part[:, 1:2])
-            along_z = wrapped(point_z - part[:, 2:3])
-            factor_x = jnp.exp(rate * along_x * along_x)
-            factor_yz = jnp.exp(rate * along_y * along_y) * jnp.exp(rate * along_z * along_z)
+            part = slice(h * HALF, (h + 1) * HALF)
             start = pl.multiple_of(a * FB + h * HALF, HALF)
             for i in range(SIDE):
                 orb_ref[pl.ds(start, HALF), i * LAYER : (i + 1) * LAYER] = (
-                    factor_x[:, i : i + 1] * factor_yz
+                    factor_x[part, i : i + 1] * factor_yz[part]
                 ).astype(bf16)
         return carry
 
@@ -89,16 +88,36 @@
 
 
 def density_kernel(
-    devices, bb_ref, rows_hbm, cx, cy, cz, ex, pd_ref, sum_ref, rows_vmem, orb_ref, mat_ref, tmp_ref, sel_ref, sem
+    devices,
+    bb_ref,
+    rows_hbm,
+    cx,
+    cy,
+    cz,
+    ex,
+    pd_ref,
+    sum_ref,
+    orb_hbm,
+    rows_vmem,
+    orb_all,
+    mat_ref,
+    tmp_ref,
+    sel_ref,
+    sem,
+    orb_sem,
 ):
     me = lax.axis_index("dev")
     load = pltpu.make_async_copy(rows_hbm, rows_vmem, sem)
     load.start()
-    tmp_ref[...] = jnp.zeros_like(tmp_ref)
+
+    def keep(t):
+        return pltpu.make_async_copy(orb_all.at[t], orb_hbm.at[t], orb_sem.at[t])
 
     def one_brick(t, carry):
         brick = lax.rem(me + t - 1 + devices, devices)
+        orb_ref = orb_all.at[t]
         fill_orbitals(brick, devices, bb_ref, (cx, cy, cz, ex), tmp_ref, orb_ref)
+        keep(t).start()
         count = find_slots(brick, me, bb_ref, sel_ref)
 
         @pl.when(t == 0)
@@ -137,6 +156,8 @@
     lax.fori_loop(0, 3, one_brick, 0)
     layer = jnp.sum(pd_ref[0] + pd_ref[1] + pd_ref[2], axis=0, keepdims=True)
     sum_ref[0] = layer[:, :FB] + layer[:, FB:]
+    for t in range(3):
+        keep(t).wait()
 
 
 def potential_kernel(
@@ -235,9 +256,14 @@
         out_ref[t] = two - slater * root
 
 
-def ham_kernel(devices, bb_ref, pot_ref, cx, cy, cz, ex, out_hbm, acc_ref, orb_ref, wei_ref, tmp_ref, sel_ref, sem):
+def ham_kernel(devices, bb_ref, pot_ref, orb_hbm, out_hbm, acc_ref, orb_all, wei_ref, sel_ref, sem, orb_sem):
     me = lax.axis_index("dev")
-    tmp_ref[...] = jnp.zeros_like(tmp_ref)
+
+    def fetch(t):
+        return pltpu.make_async_copy(orb_hbm.at[t], orb_all.at[t], orb_sem.at[t])
+
+    for t in range(3):
+        fetch(t).start()
 
     def clear(r, carry):
         acc_ref[pl.ds(pl.multiple_of(r * 64, 64), 64), :] = jnp.zeros((64, COLS), f32)
@@ -247,8 +273,9 @@
 
     def one_brick(t, carry):
         brick = lax.rem(me + t - 1 + devices, devices)
-        fill_orbitals(brick, devices, bb_ref, (cx, cy, cz, ex), tmp_ref, orb_ref)
+        orb_ref = orb_all.at[t]
         count = find_slots(brick, me, bb_ref, sel_ref)
+        fetch(t).wait()
 
         def weigh(k, inner):
             source = pl.multiple_of(sel_ref[k] * FB, FB)
@@ -295,18 +322,23 @@
     smem = pl.BlockSpec(memory_space=pltpu.SMEM)
     anywhere = pl.BlockSpec(memory_space=pl.ANY)
     grid = (3, SIDE, LAYER)
-    partial, sums = pl.pallas_call(
+    partial, sums, orbitals = pl.pallas_call(
         functools.partial(density_kernel, devices),
-        out_shape=(jax.ShapeDtypeStruct(grid, f32), jax.ShapeDtypeStruct((1, 1, FB), f32)),
+        out_shape=(
+            jax.ShapeDtypeStruct(grid, f32),
+            jax.ShapeDtypeStruct((1, 1, FB), f32),
+            jax.ShapeDtypeStruct((3, KB * FB, CELLS), bf16),
+        ),
         in_specs=[smem, anywhere] + [vmem] * 4,
-        out_specs=(vmem, vmem),
+        out_specs=(vmem, vmem, anywhere),
         scratch_shapes=[
             pltpu.VMEM((ROWS, COLS), bf16),
-            pltpu.VMEM((KB * FB, CELLS), bf16),
+            pltpu.VMEM((3, KB * FB, CELLS), bf16),
             pltpu.VMEM((CAP * FB, KB * FB), bf16),
-            pltpu.VMEM((8, FB), f32),
+            pltpu.VMEM((LAYER, FB), f32),
             pltpu.SMEM((CAP,), jnp.int32),
             pltpu.SemaphoreType.DMA,
+            pltpu.SemaphoreType.DMA((3,)),
         ],
         compiler_params=pltpu.CompilerParams(vmem_limit_bytes=VMEM_BYTES),
         name="partial_density",
@@ -334,19 +366,19 @@
     ham = pl.pallas_call(
         functools.partial(ham_kernel, devices),
         out_shape=jax.ShapeDtypeStruct((ROWS, COLS), f32),
-        in_specs=[smem] + [vmem] * 5,
+        in_specs=[smem, vmem, anywhere],
         out_specs=anywhere,
         scratch_shapes=[
             pltpu.VMEM((ROWS, COLS), f32),
-            pltpu.VMEM((KB * FB, CELLS), bf16),
+            pltpu.VMEM((3, KB * FB, CELLS), bf16),
             pltpu.VMEM((CAP * FB, CELLS), bf16),
-            pltpu.VMEM((8, FB), f32),
             pltpu.SMEM((CAP,), jnp.int32),
             pltpu.SemaphoreType.DMA,
+            pltpu.SemaphoreType.DMA((3,)),
         ],
         compiler_params=pltpu.CompilerParams(vmem_limit_bytes=VMEM_BYTES),
         name="ham_rows",
-    )(brick_blocks, potentials, *params)
+    )(brick_blocks, potentials, orbitals)
     return potentials[1].reshape(1, CELLS), ham
 
 

time: 100 us -> 78.3 us (0.78)
  Pallas kernels: 96.1 us -> 74.6 us
    pallas_call x1, Pallas kernels: 43.9 us -> 27.5 us  [local(): pl.pallas_call(functools.partial(ham_kernel, devices), out_shape=jax.Shap...]
    pallas_call x1, Pallas kernels: 39 us -> 33.3 us  [local(): pl.pallas_call(functools.partial(density_kernel, devices), out_shape=(jax...]
where the time goes in v2:
time: 78.3 us; the launch traced here: 77.9 us
  Pallas kernels  74.6 us (95%)
  local copies, waits for them, and re-layouts  2.71 us (3%)
    pallas_call x1, Pallas kernels, local(): pl.pallas_call(functools.partial(density_kernel, devices), out_shape=(jax...  33.3 us
    pallas_call x1, Pallas kernels, local(): pl.pallas_call(functools.partial(ham_kernel, devices), out_shape=jax.Shap...  27.5 us
    pallas_call x1, Pallas kernels, local(): pl.pallas_call(functools.partial(potential_kernel, devices), out_shape=ja...  13.8 us
    unnamed x3, local copies, waits for them, and re-layouts  2.71 us

profile of v2, /device:TPU:0, one launch (start us, length us, event | category | flops | bytes accessed | tf_op | source)
XLA Modules:
  0.0 77.9 jit_solution(9135586207155241165)
XLA Ops:
  0.6 1.4 %copy.8.bb_ref = s32[32,8]{1,0:T(8,128)} copy(s32[32,8]{0,1:T(8,128)} %param.11) | data formatting | bytes 2048 | tf_op args[5]
  2.0 33.3 %partial_density.1 = (f32[3,16,256]{2,1,0:T(8,128)}, f32[1,1,128]{2,1,0:T(1,128)}, bf16[3,1024,4096]{2,1,0:T(8,128)(2,1)}) custom-call(s32[32,8]{1,0:T(8,128)} %copy.8.bb_ref, bf16[768,3840]{1,0:T(8,128)(2,1)} %rows_hbm.1, f32[192,128]{1,0:T(8,128)} %bitcast.7, f32[192,128]{1,0:T(8,128)} %bitcast.8, f32[192,128]{1,0:T(8,128)} %bitcast.9, f32[192,128]{1,0:T(8,128)} %bitcast.10), custom_call_target="tpu_custom_call" | custom-call | tf_op jit(solution)/shard_map/partial_density/pallas_call | solution.py:325
  35.3 13.8 %exchange_potential.1.pot_ref = f32[3,16,256]{2,1,0:T(8,128)} custom-call(f32[3,16,256]{2,1,0:T(8,128)} %get-tuple-element.5.pd_ref, f32[1,1,128]{2,1,0:T(1,128)} %get-tuple-element.6.sum_ref), custom_call_target="tpu_custom_call" | custom-call | tf_op jit(solution)/shard_map/exchange_potential/pallas_call | solution.py:346
  49.1 27.5 %ham_rows.1 = f32[768,3840]{1,0:T(8,128)} custom-call(s32[32,8]{1,0:T(8,128)} %copy.8.bb_ref, f32[3,16,256]{2,1,0:T(8,128)} %exchange_potential.1.pot_ref, bf16[3,1024,4096]{2,1,0:T(8,128)(2,1)} %get-tuple-element.7.orb_hbm), custom_call_target="tpu_custom_call" | custom-call | tf_op jit(solution)/shard_map/ham_rows/pallas_call | solution.py:366
  76.6 0.7 slice_bitcast_fusion
  77.3 0.6 copy.10
